TPU v7x, 32 devices: a whole 2x2x4 slice. The times are simulated.
32 devices in a mesh: sp: 2 (over x), ep: 16 (over z, y, core).
Axes of the slice: x: 2, y: 2, z: 4, core: 2. Of those that a mesh axis runs over, the one named last changes fastest.
Arguments:
- activations: bfloat16 [16, 8, 3584], P('ep', 'sp'), may hold values from -6 to 6
- out_grad: bfloat16 [16, 8, 3584], P('ep', 'sp'), may hold values from -6 to 6
- route_weights: bfloat16 [16, 8, 8], P('ep', 'sp'), may hold values from 0.019897461 to 0.5
- expert_ids: int32 [16, 8, 8], P('ep', 'sp'), may hold values from 0 to 15, all different within a row; in each aligned block of 8 rows (0 to 7, 8 to 15, ..., all dimensions but the last counted through in order) at most 6 rows name the same one
- w_gate: bfloat16 [16, 3584, 1024], P('ep', None, 'sp'), may hold values from -0.09375 to 0.09375
- w_up: bfloat16 [16, 3584, 1024], P('ep', None, 'sp'), may hold values from -0.09375 to 0.09375
- w_down: bfloat16 [16, 1024, 3584], P('ep', 'sp'), may hold values from -0.1875 to 0.1875
Outputs:
- input_grad: bfloat16 [16, 8, 3584], P('ep', 'sp')
- w_down_grad: float32 [16, 1024, 3584], P('ep', 'sp')
Inputs may be any that keep to these rules, and one draw needn't show every extreme that they name: `expert_ids`: each row names 8 different experts. In each aligned block of 8 rows (one token group, the first two dimensions taken together) no expert is named by more than 6 rows, a bound that some block reaches.
All inputs are finite; a program needn't handle non-finite values.
Results may differ from a plain program's by a relative error of at most 0.014.
Values may be sent and summed in bfloat16 or wider, within the bound.
No kernel may reach another device: no remote copies, remote signals or barrier semaphores. Data moves between devices by JAX's collectives and lax.ppermute only.
A program may use at most 64 MiB of HBM per device.

v0:
```python
import jax
import jax.numpy as jnp
from jax import lax
from jax.sharding import PartitionSpec as P

TOP = 8


def expert_rows(rows_in, rows_grad, gate_w, up_w, down_w):
    gate_pre = jnp.dot(rows_in, gate_w, preferred_element_type=jnp.float32)
    up_pre = jnp.dot(rows_in, up_w, preferred_element_type=jnp.float32)
    squash = jax.nn.sigmoid(gate_pre)
    swish = gate_pre * squash
    hidden = (swish * up_pre).astype(jnp.bfloat16)
    hidden_grad = lax.dot_general(
        rows_grad, down_w, (((1,), (1,)), ((), ())), preferred_element_type=jnp.float32
    )
    gate_grad = (hidden_grad * up_pre * squash * (1.0 + gate_pre * (1.0 - squash))).astype(
        jnp.bfloat16
    )
    up_grad = (hidden_grad * swish).astype(jnp.bfloat16)
    first = lax.dot_general(
        gate_grad, gate_w, (((1,), (1,)), ((), ())), preferred_element_type=jnp.float32
    )
    second = lax.dot_general(
        up_grad, up_w, (((1,), (1,)), ((), ())), preferred_element_type=jnp.float32
    )
    partial_rows = (first + second).astype(jnp.bfloat16)
    weight_grad = lax.dot_general(
        hidden, rows_grad, (((0,), (0,)), ((), ())), preferred_element_type=jnp.float32
    )
    return (partial_rows, weight_grad)


def per_device(activations, out_grad, route_weights, expert_ids, w_gate, w_up, w_down):
    n_expert = lax.axis_size("ep")
    n_group = lax.axis_size("sp")
    tok_dev = activations.shape[1]
    width = activations.shape[2]
    capacity = max(2, tok_dev * n_group * TOP * 3 // (2 * n_expert))
    group_ids = lax.all_gather(expert_ids, "sp", axis=1, tiled=True)
    group_in, group_grad, group_weight = (
        lax.all_gather(activations, "sp", axis=1, tiled=True),
        lax.all_gather(out_grad, "sp", axis=1, tiled=True),
        lax.all_gather(route_weights, "sp", axis=1, tiled=True),
    )
    send_width = group_in.shape[2]
    tok_grp = group_ids.shape[1]
    slot_expert = group_ids[0].reshape(-1)
    slot_token = jnp.arange(slot_expert.shape[0], dtype=jnp.int32) // TOP
    onehot = (slot_expert[:, None] == jnp.arange(n_expert, dtype=jnp.int32)[None, :]).astype(
        jnp.int32
    )
    before = jnp.cumsum(onehot, axis=0) - onehot
    rank = jnp.sum(before * onehot, axis=1)
    position = slot_expert * capacity + rank
    total_rows = n_expert * capacity
    token_in = group_in[0][slot_token]
    scaled = (
        group_weight[0].reshape(-1).astype(jnp.float32)[:, None]
        * group_grad[0][slot_token].astype(jnp.float32)
    ).astype(jnp.bfloat16)
    send_in = (
        jnp.zeros((total_rows, send_width), jnp.bfloat16)
        .at[position]
        .set(token_in)
        .reshape(n_expert, capacity, send_width)
    )
    send_grad = (
        jnp.zeros((total_rows, send_width), jnp.bfloat16)
        .at[position]
        .set(scaled)
        .reshape(n_expert, capacity, send_width)
    )
    recv_in, recv_grad = (
        lax.all_to_all(send_in, "ep", split_axis=0, concat_axis=0, tiled=True),
        lax.all_to_all(send_grad, "ep", split_axis=0, concat_axis=0, tiled=True),
    )
    flat_in = recv_in.reshape(total_rows, width)
    flat_grad = recv_grad.reshape(total_rows, width)
    gate_w = w_gate[0]
    up_w = w_up[0]
    down_w = w_down[0]
    partial_rows, weight_grad = expert_rows(flat_in, flat_grad, gate_w, up_w, down_w)
    partial_rows = partial_rows.reshape(n_expert, capacity, width)
    slot_owner = jnp.full((total_rows,), -1, jnp.int32).at[position].set(slot_token)
    owner_match = jnp.arange(tok_grp, dtype=jnp.int32)[:, None] == slot_owner[None, :]
    back_rows = lax.all_to_all(partial_rows, "ep", split_axis=0, concat_axis=0, tiled=True)
    token_sum = jnp.dot(
        owner_match.astype(jnp.bfloat16),
        back_rows.reshape(total_rows, width),
        preferred_element_type=jnp.float32,
    )
    own_sum = lax.psum_scatter(
        token_sum.astype(jnp.bfloat16), "sp", scatter_dimension=0, tiled=True
    )
    return (own_sum.reshape(1, tok_dev, width), weight_grad[None])


def solution(mesh):
    return jax.shard_map(
        per_device,
        mesh=mesh,
        in_specs=(
            P("ep", "sp", None),
            P("ep", "sp", None),
            P("ep", "sp", None),
            P("ep", "sp", None),
            P("ep", None, "sp"),
            P("ep", None, "sp"),
            P("ep", "sp", None),
        ),
        out_specs=(P("ep", "sp", None), P("ep", "sp", None)),
        check_vma=False,
    )
```

profile of v0, /device:TPU:16, one launch (start us, length us, event | category | flops | bytes accessed | tf_op | source)
XLA Modules:
  0.0 116.9 jit_solution(2344344698198534478)
XLA Ops:
  0.6 0.0 copy-start.4
  0.6 0.0 copy-start.3
  0.7 4.5 %all_gather.12 = s32[1,8,8]{2,0,1:T(1,128)S(1)} all-gather(s32[1,4,8]{2,0,1:T(1,128)} %bitcast.44), channel_id=1, replica_groups=mesh['sp'=2,'ep'=16] {'sp'}, dimensions={1}, use_global_device_ids=true | all-gather | bytes 384 | tf_op jit(solution)/shard_map/all_gather | solution.py:41
  5.2 0.5 broadcast.143
  5.7 0.7 fusion.30
  6.4 0.1 eq.29
  6.5 0.1 mul.50
  6.5 0.1 fusion.20
  6.6 0.1 reduce_window_sum.11
  6.7 0.2 select_reduce_fusion
  6.9 0.8 copy.16
  7.7 4.8 %all_gather.15 = bf16[1,8,3584]{2,0,1:T(2,128)(2,1)S(1)} all-gather(bf16[1,4,3584]{2,0,1:T(2,128)(2,1)S(1)} %copy.16), channel_id=1, replica_groups=mesh['sp'=2,'ep'=16] {'sp'}, dimensions={1}, use_global_device_ids=true | all-gather | bytes 86016 | tf_op jit(solution)/shard_map/all_gather | solution.py:43
  12.6 2.8 %scatter_custom_fusion.2 = bf16[96,3584]{1,0:T(8,128)(2,1)S(1)} fusion(s32[64]{0:T(128)S(1)} %fusion.23, bf16[8,3584]{1,0:T(8,128)(2,1)S(1)} %bitcast.43, s32[1024]{0:T(1024)S(1)} %pad_clamp_fusion, bf16[]{:T(256)} %constant.34.clone.1), kind=kCustom, calls=%fused_computation.20 | custom fusion | bytes 688130 | tf_op jit(solution)/shard_map/scatter | solution.py:66
  15.4 1.2 reshape.107
  16.5 6.2 %all-to-all-start.1 = ((bf16[16,6,3584]{2,1,0:T(8,128)(2,1)}), bf16[16,6,3584]{2,1,0:T(8,128)(2,1)S(1)}, u32[]{:S(2)}, u32[]{:S(2)}) async-start(bf16[16,6,3584]{2,1,0:T(8,128)(2,1)} %reshape.107), calls=%async_computation.1 | async-start | bytes 1835008 | tf_op jit(solution)/shard_map/all_to_all | solution.py:76
  22.7 0.0 copy-done.4
  22.7 4.4 %all_gather.13 = bf16[1,8,8]{2,0,1:T(2,128)(2,1)S(1)} all-gather(bf16[1,4,8]{2,0,1:T(2,128)(2,1)S(1)} %copy.14), channel_id=1, replica_groups=mesh['sp'=2,'ep'=16] {'sp'}, dimensions={1}, use_global_device_ids=true | all-gather | bytes 192 | tf_op jit(solution)/shard_map/all_gather | solution.py:45
  27.1 0.1 reshape.112
  27.2 0.0 copy-done.3
  27.2 4.8 %all_gather.14 = bf16[1,8,3584]{2,0,1:T(2,128)(2,1)S(1)} all-gather(bf16[1,4,3584]{2,0,1:T(2,128)(2,1)S(1)} %copy.15), channel_id=1, replica_groups=mesh['sp'=2,'ep'=16] {'sp'}, dimensions={1}, use_global_device_ids=true | all-gather | bytes 86016 | tf_op jit(solution)/shard_map/all_gather | solution.py:44
  32.1 2.9 %scatter_custom_fusion.1 = bf16[96,3584]{1,0:T(8,128)(2,1)S(1)} fusion(s32[64]{0:T(128)S(1)} %fusion.23, f32[64]{0:T(128)S(1)} %reshape.112, bf16[]{:T(256)} %constant.34.clone.1, bf16[8,3584]{1,0:T(8,128)(2,1)S(1)} %bitcast.42, s32[1024]{0:T(1024)S(1)} %pad_clamp_fusion), kind=kCustom, calls=%fused_computation.19 | custom fusion | flops 688128 | bytes 750082 | tf_op jit(solution)/shard_map/scatter | solution.py:72
  35.0 1.2 reshape.105
  36.1 8.9 %all-to-all-done.1 = bf16[16,6,3584]{2,1,0:T(8,128)(2,1)S(1)} async-done(((bf16[16,6,3584]{2,1,0:T(8,128)(2,1)}), bf16[16,6,3584]{2,1,0:T(8,128)(2,1)S(1)}, u32[]{:S(2)}, u32[]{:S(2)}) %all-to-all-start.1) | async-done | bytes 688160 | tf_op jit(solution)/shard_map/all_to_all | solution.py:76
  45.0 4.5 %all-to-all-start = ((bf16[16,6,3584]{2,1,0:T(8,128)(2,1)}), bf16[16,6,3584]{2,1,0:T(8,128)(2,1)S(1)}, u32[]{:S(2)}, u32[]{:S(2)}) async-start(bf16[16,6,3584]{2,1,0:T(8,128)(2,1)} %reshape.105), calls=%async_computation | async-start | bytes 1835008 | tf_op jit(solution)/shard_map/all_to_all | solution.py:77
  49.6 0.2 reshape.108
  49.8 0.0 copy-start.1
  49.8 2.9 %fusion.3 = f32[96,512]{1,0:T(8,128)S(1)} fusion(bf16[96,3584]{1,0:T(8,128)(2,1)S(1)} %reshape.108, bf16[1,3584,512]{2,1,0:T(8,128)(2,1)} %param.11), kind=kOutput, calls=%fused_computation.11 | convolution fusion | flops 352321536 | bytes 4554752 | tf_op jit(solution)/shard_map/dot_general | solution.py:10
  52.7 0.2 copy-done.1
  53.0 0.7 fusion.6
  53.7 18.2 %all-to-all-done = bf16[16,6,3584]{2,1,0:T(8,128)(2,1)S(1)} async-done(((bf16[16,6,3584]{2,1,0:T(8,128)(2,1)}), bf16[16,6,3584]{2,1,0:T(8,128)(2,1)S(1)}, u32[]{:S(2)}, u32[]{:S(2)}) %all-to-all-start) | async-done | bytes 688160 | tf_op jit(solution)/shard_map/all_to_all | solution.py:77
  71.9 0.2 reshape.106
  72.1 0.0 copy-start
  72.2 3.4 %fusion.8 = f32[96,512]{1,0:T(8,128)S(1)} fusion(bf16[96,3584]{1,0:T(8,128)(2,1)S(1)} %reshape.106, bf16[1,512,3584]{2,1,0:T(8,128)(2,1)} %param.13), kind=kOutput, calls=%fused_computation.16 | convolution fusion | flops 352321536 | bytes 4554752 | tf_op jit(solution)/shard_map/dot_general | solution.py:15
  75.6 0.0 copy-done
  75.6 0.0 copy-start.2
  75.6 1.2 %fusion.1 = f32[96,3584]{1,0:T(8,128)S(1)} fusion(bf16[1,3584,512]{2,1,0:T(8,128)(2,1)S(1)} %copy-done, f32[96,512]{1,0:T(8,128)S(1)} %fusion.3, f32[96,512]{1,0:T(8,128)S(1)} %fusion.8, f32[96,512]{1,0:T(8,128)S(1)} %fusion.6), kind=kOutput, calls=%fused_computation.9 | convolution fusion | flops 352813056 | bytes 5636096 | tf_op jit(solution)/shard_map/dot_general | solution.py:22
  76.8 0.8 copy-done.2
  77.6 1.2 %fusion = bf16[96,3584]{1,0:T(8,128)(2,1)S(1)} fusion(f32[96,3584]{1,0:T(8,128)S(1)} %fusion.1, bf16[1,3584,512]{2,1,0:T(8,128)(2,1)S(1)} %copy-done.2, f32[96,512]{1,0:T(8,128)S(1)} %fusion.8, f32[96,512]{1,0:T(8,128)S(1)} %fusion.3), kind=kOutput, calls=%fused_computation.7 | convolution fusion | flops 353304576 | bytes 6127616 | tf_op jit(solution)/shard_map/dot_general | solution.py:25
  78.9 1.2 reshape.109
  80.0 4.5 %all-to-all-start.2 = ((bf16[16,6,3584]{2,1,0:T(8,128)(2,1)}), bf16[16,6,3584]{2,1,0:T(8,128)(2,1)S(1)}, u32[]{:S(2)}, u32[]{:S(2)}) async-start(bf16[16,6,3584]{2,1,0:T(8,128)(2,1)} %reshape.109), calls=%async_computation.2 | async-start | bytes 1835008 | tf_op jit(solution)/shard_map/all_to_all | solution.py:88
  84.6 0.6 dynamic-slice
  85.8 0.8 scatter_custom_fusion
  86.6 4.2 %convolution_bitcast_fusion = f32[1,512,3584]{2,1,0:T(8,128)} fusion(bf16[96,3584]{1,0:T(8,128)(2,1)S(1)} %reshape.106, f32[96,512]{1,0:T(8,128)S(1)} %fusion.6, f32[96,512]{1,0:T(8,128)S(1)} %fusion.3), kind=kOutput, calls=%fused_computation.5 | convolution fusion | flops 352616448 | bytes 8421376 | tf_op jit(solution)/shard_map/dot_general | solution.py:29
  90.8 16.1 %all-to-all-done.2 = bf16[16,6,3584]{2,1,0:T(8,128)(2,1)S(1)} async-done(((bf16[16,6,3584]{2,1,0:T(8,128)(2,1)}), bf16[16,6,3584]{2,1,0:T(8,128)(2,1)S(1)}, u32[]{:S(2)}, u32[]{:S(2)}) %all-to-all-start.2) | async-done | bytes 688160 | tf_op jit(solution)/shard_map/all_to_all | solution.py:88
  106.9 0.2 reshape.110
  107.1 0.2 convolution_convert_fusion
  107.3 9.0 %all-reduce = bf16[8,3584]{1,0:T(8,128)(2,1)S(1)} all-reduce(bf16[8,3584]{1,0:T(8,128)(2,1)S(1)} %convolution_convert_fusion), channel_id=2, replica_groups=mesh['sp'=2,'ep'=16] {'sp'}, use_global_device_ids=true, to_apply=%region_5.6.clone | all-reduce | flops 28672 | bytes 114688
  116.3 0.6 dynamic-slice_bitcast_fusion
  (11 shorter events, 0.1 us)
Async XLA Ops:
  0.6 22.1 %copy-start.4 = (bf16[1,4,8]{2,1,0:T(4,128)(2,1)S(1)}, bf16[1,4,8]{2,1,0:T(4,128)(2,1)}, u32[]{:S(2)}) copy-start(bf16[1,4,8]{2,1,0:T(4,128)(2,1)} %param.9) | copy-start | bytes 196
  0.6 26.6 %copy-start.3 = (bf16[1,4,3584]{2,1,0:T(4,128)(2,1)S(1)}, bf16[1,4,3584]{2,1,0:T(4,128)(2,1)}, u32[]{:S(2)}) copy-start(bf16[1,4,3584]{2,1,0:T(4,128)(2,1)} %param.8) | copy-start | bytes 86020
  16.5 28.5 %all-to-all-start.1 = ((bf16[16,6,3584]{2,1,0:T(8,128)(2,1)}), bf16[16,6,3584]{2,1,0:T(8,128)(2,1)S(1)}, u32[]{:S(2)}, u32[]{:S(2)}) async-start(bf16[16,6,3584]{2,1,0:T(8,128)(2,1)} %reshape.107), calls=%async_computation.1 | async-start | bytes 1835008 | tf_op jit(solution)/shard_map/all_to_all | solution.py:76
  45.0 26.9 %all-to-all-start = ((bf16[16,6,3584]{2,1,0:T(8,128)(2,1)}), bf16[16,6,3584]{2,1,0:T(8,128)(2,1)S(1)}, u32[]{:S(2)}, u32[]{:S(2)}) async-start(bf16[16,6,3584]{2,1,0:T(8,128)(2,1)} %reshape.105), calls=%async_computation | async-start | bytes 1835008 | tf_op jit(solution)/shard_map/all_to_all | solution.py:77
  49.8 3.1 %copy-start.1 = (bf16[1,3584,512]{2,1,0:T(8,128)(2,1)S(1)}, bf16[1,3584,512]{2,1,0:T(8,128)(2,1)}, u32[]{:S(2)}) copy-start(bf16[1,3584,512]{2,1,0:T(8,128)(2,1)} %param.12) | copy-start | bytes 11010052
  72.1 3.4 %copy-start = (bf16[1,3584,512]{2,1,0:T(8,128)(2,1)S(1)}, bf16[1,3584,512]{2,1,0:T(8,128)(2,1)}, u32[]{:S(2)}) copy-start(bf16[1,3584,512]{2,1,0:T(8,128)(2,1)} %param.11) | copy-start | bytes 11010052
  75.6 2.0 %copy-start.2 = (bf16[1,3584,512]{2,1,0:T(8,128)(2,1)S(1)}, bf16[1,3584,512]{2,1,0:T(8,128)(2,1)}, u32[]{:S(2)}) copy-start(bf16[1,3584,512]{2,1,0:T(8,128)(2,1)} %param.12) | copy-start | bytes 11010052
  77.6 7.0 %copy-start.5 = (u32[32]{0:T(128)S(1)}, u32[32]{0:T(128)}, u32[]{:S(2)}) copy-start(u32[32]{0:T(128)} %constant.46) | copy-start | bytes 388
  80.0 26.9 %all-to-all-start.2 = ((bf16[16,6,3584]{2,1,0:T(8,128)(2,1)}), bf16[16,6,3584]{2,1,0:T(8,128)(2,1)S(1)}, u32[]{:S(2)}, u32[]{:S(2)}) async-start(bf16[16,6,3584]{2,1,0:T(8,128)(2,1)} %reshape.109), calls=%async_computation.2 | async-start | bytes 1835008 | tf_op jit(solution)/shard_map/all_to_all | solution.py:88
where the time goes:
time: 118 us; the launch traced here: 117 us
  waiting for transfers between devices  43.3 us (37%)
  blocking collectives  27.5 us (23%)
  starting transfers between devices  15.3 us (13%)
  matrix products  13.9 us (12%)
  local copies, waits for them, and re-layouts  11.6 us (10%)
  other arithmetic  3.92 us (3%)
  between operations  1.49 us (1%)
    all_to_all x1, waiting for transfers between devices, per_device(): lax.all_to_all(send_grad, 'ep', split_axis=0, concat_axis=0, tiled=True)  18.2 us
    all_to_all x1, waiting for transfers between devices, per_device(): lax.all_to_all(partial_rows, 'ep', split_axis=0, concat_axis=0, tiled=True)  16.1 us
    unnamed x1, blocking collectives  8.96 us
    all_to_all x1, waiting for transfers between devices, per_device(): lax.all_to_all(send_in, 'ep', split_axis=0, concat_axis=0, tiled=True)  8.92 us
    all_to_all x1, starting transfers between devices, per_device(): lax.all_to_all(send_in, 'ep', split_axis=0, concat_axis=0, tiled=True)  6.18 us
    all_gather x1, blocking collectives, per_device(): lax.all_gather(activations, 'sp', axis=1, tiled=True)  4.85 us
    all_gather x1, blocking collectives, per_device(): lax.all_gather(out_grad, 'sp', axis=1, tiled=True)  4.85 us
    all_to_all x1, starting transfers between devices, per_device(): lax.all_to_all(send_grad, 'ep', split_axis=0, concat_axis=0, tiled=True)  4.53 us
  transfers between devices with their start and end apart: 3, of which 3 were waited for; matrix products, arithmetic and copies ran while one was open for 12% of the time, Pallas kernels for 0%

commit v1 on v0

--- a/solution.py
+++ b/solution.py
@@ -72,8 +72,30 @@
         .set(scaled)
         .reshape(n_expert, capacity, send_width)
     )
+
+    def shapes_unite(state, axis_tag="ep"):
+        part_now = lax.axis_size(axis_tag)
+        lower = lax.axis_index(axis_tag)
+        e_now, main = (part_now, lower)
+        inter = list(state.shape)
+        placed = state.shape[0] // e_now
+        inter[0] = placed
+        n_now = inter[0]
+        inter[0] = n_now * e_now
+        taken_in = jnp.zeros(inter, state.dtype)
+        for b in range(e_now):
+            work_now = lax.dynamic_slice_in_dim(state, (main ^ b) * placed, placed, axis=0)
+            if b:
+                work_now = lax.ppermute(
+                    work_now, axis_tag, [(hop_no, hop_no ^ b) for hop_no in range(e_now)]
+                )
+            taken_in = lax.dynamic_update_slice_in_dim(
+                taken_in, work_now, (main ^ b) * n_now, axis=0
+            )
+        return taken_in
+
     recv_in, recv_grad = (
-        lax.all_to_all(send_in, "ep", split_axis=0, concat_axis=0, tiled=True),
+        shapes_unite(send_in),
         lax.all_to_all(send_grad, "ep", split_axis=0, concat_axis=0, tiled=True),
     )
     flat_in = recv_in.reshape(total_rows, width)

time: 118 us -> 149 us (1.26)
  starting transfers between devices: 15.3 us -> 36.7 us
  waiting for transfers between devices: 43.3 us -> 53 us
    ppermute x0 -> x15, waiting for transfers between devices: none -> 36.9 us  [shapes_unite(): lax.ppermute(work_now, axis_tag, [(hop_no, hop_no ^ b) for hop_no in rang...]
    ppermute x0 -> x15, starting transfers between devices: none -> 24.1 us  [shapes_unite(): lax.ppermute(work_now, axis_tag, [(hop_no, hop_no ^ b) for hop_no in rang...]
    all_to_all x1, waiting for transfers between devices: 18.2 us -> 0.01 us  [per_device(): lax.all_to_all(send_grad, 'ep', split_axis=0, concat_axis=0, tiled=True)]
    all_to_all x1 -> x0, waiting for transfers between devices: 8.92 us -> none  [per_device(): lax.all_to_all(send_in, 'ep', split_axis=0, concat_axis=0, tiled=True)]
    all_to_all x1 -> x0, starting transfers between devices: 6.18 us -> none  [per_device(): lax.all_to_all(send_in, 'ep', split_axis=0, concat_axis=0, tiled=True)]
    all_to_all x1, starting transfers between devices: 4.53 us -> 6.44 us  [per_device(): lax.all_to_all(partial_rows, 'ep', split_axis=0, concat_axis=0, tiled=True)]
    all_to_all x1, starting transfers between devices: 4.53 us -> 6.18 us  [per_device(): lax.all_to_all(send_grad, 'ep', split_axis=0, concat_axis=0, tiled=True)]
    unnamed x18 -> x16, local copies, waits for them, and re-layouts: 2.5 us -> 3.17 us
  transfers between devices with their start and end apart: 3 -> 17, of which waited for: 3 -> 11; matrix products, arithmetic and copies ran while one was open for 12% -> 9% of each run, Pallas kernels for 0% -> 0%
where the time goes in v1:
time: 149 us; the launch traced here: 148 us
  waiting for transfers between devices  53 us (36%)
  starting transfers between devices  36.7 us (25%)
  blocking collectives  27.5 us (18%)
  matrix products  13.9 us (9%)
  local copies, waits for them, and re-layouts  11.7 us (8%)
  other arithmetic  3.91 us (3%)
  between operations  1.75 us (1%)
    ppermute x15, waiting for transfers between devices, shapes_unite(): lax.ppermute(work_now, axis_tag, [(hop_no, hop_no ^ b) for hop_no in rang...  36.9 us
    ppermute x15, starting transfers between devices, shapes_unite(): lax.ppermute(work_now, axis_tag, [(hop_no, hop_no ^ b) for hop_no in rang...  24.1 us
    all_to_all x1, waiting for transfers between devices, per_device(): lax.all_to_all(partial_rows, 'ep', split_axis=0, concat_axis=0, tiled=True)  16.1 us
    unnamed x1, blocking collectives  8.96 us
    all_to_all x1, starting transfers between devices, per_device(): lax.all_to_all(partial_rows, 'ep', split_axis=0, concat_axis=0, tiled=True)  6.44 us
    all_to_all x1, starting transfers between devices, per_device(): lax.all_to_all(send_grad, 'ep', split_axis=0, concat_axis=0, tiled=True)  6.18 us
    all_gather x1, blocking collectives, per_device(): lax.all_gather(activations, 'sp', axis=1, tiled=True)  4.85 us
    all_gather x1, blocking collectives, per_device(): lax.all_gather(out_grad, 'sp', axis=1, tiled=True)  4.85 us
  transfers between devices with their start and end apart: 17, of which 11 were waited for; matrix products, arithmetic and copies ran while one was open for 9% of the time, Pallas kernels for 0%

profile of v1, /device:TPU:16, one launch (start us, length us, event | category | flops | bytes accessed | tf_op | source)
XLA Modules:
  0.0 148.4 jit_solution(7617024376013938534)
XLA Ops:
  0.7 0.7 copy.14
  1.4 4.5 %all_gather.12 = s32[1,8,8]{2,0,1:T(1,128)S(1)} all-gather(s32[1,4,8]{2,0,1:T(1,128)} %bitcast.44), channel_id=1, replica_groups=mesh['sp'=2,'ep'=16] {'sp'}, dimensions={1}, use_global_device_ids=true | all-gather | bytes 384 | tf_op jit(solution)/shard_map/all_gather | solution.py:41
  5.9 0.5 broadcast.151
  6.4 0.7 fusion.30
  7.6 0.8 copy.16
  8.4 4.8 %all_gather.15 = bf16[1,8,3584]{2,0,1:T(2,128)(2,1)S(1)} all-gather(bf16[1,4,3584]{2,0,1:T(2,128)(2,1)S(1)} %copy.16), channel_id=1, replica_groups=mesh['sp'=2,'ep'=16] {'sp'}, dimensions={1}, use_global_device_ids=true | all-gather | bytes 86016 | tf_op jit(solution)/shard_map/all_gather | solution.py:43
  13.3 2.8 %scatter_custom_fusion.2 = bf16[96,3584]{1,0:T(8,128)(2,1)S(1)} fusion(s32[64]{0:T(128)S(1)} %get-tuple-element.21, bf16[8,3584]{1,0:T(8,128)(2,1)S(1)} %bitcast.43, s32[1024]{0:T(1024)S(1)} %pad_clamp_fusion, bf16[]{:T(256)} %constant.16.clone.1), kind=kCustom, calls=%fused_computation.20 | custom fusion | bytes 688130 | tf_op jit(solution)/shard_map/scatter | solution.py:66
  16.1 0.2 reshape.107
  16.7 4.4 %all_gather.13 = bf16[1,8,8]{2,0,1:T(2,128)(2,1)S(1)} all-gather(bf16[1,4,8]{2,0,1:T(2,128)(2,1)S(1)} %copy.14), channel_id=1, replica_groups=mesh['sp'=2,'ep'=16] {'sp'}, dimensions={1}, use_global_device_ids=true | all-gather | bytes 192 | tf_op jit(solution)/shard_map/all_gather | solution.py:45
  21.2 4.8 %all_gather.14 = bf16[1,8,3584]{2,0,1:T(2,128)(2,1)S(1)} all-gather(bf16[1,4,3584]{2,0,1:T(2,128)(2,1)S(1)} %copy.15), channel_id=1, replica_groups=mesh['sp'=2,'ep'=16] {'sp'}, dimensions={1}, use_global_device_ids=true | all-gather | bytes 86016 | tf_op jit(solution)/shard_map/all_gather | solution.py:44
  26.1 2.9 %scatter_custom_fusion.1 = bf16[96,3584]{1,0:T(8,128)(2,1)S(1)} fusion(s32[64]{0:T(128)S(1)} %get-tuple-element.21, f32[64]{0:T(128)S(1)} %reshape.112, bf16[]{:T(256)} %constant.16.clone.1, bf16[8,3584]{1,0:T(8,128)(2,1)S(1)} %bitcast.42, s32[1024]{0:T(1024)S(1)} %pad_clamp_fusion), kind=kCustom, calls=%fused_computation.19 | custom fusion | flops 688128 | bytes 750082 | tf_op jit(solution)/shard_map/scatter | solution.py:72
  28.9 1.2 reshape.105
  30.1 6.2 %all-to-all-start = ((bf16[16,6,3584]{2,1,0:T(8,128)(2,1)}), bf16[16,6,3584]{2,1,0:T(8,128)(2,1)S(1)}, u32[]{:S(2)}, u32[]{:S(2)}) async-start(bf16[16,6,3584]{2,1,0:T(8,128)(2,1)} %reshape.105), calls=%async_computation | async-start | bytes 1835008 | tf_op jit(solution)/shard_map/all_to_all | solution.py:99
  36.3 1.2 collective-permute-start.14
  37.5 1.5 collective-permute-start.13
  38.9 0.3 collective-permute-start.12
  39.2 1.5 collective-permute-start.11
  40.7 1.5 collective-permute-start.1
  42.1 3.5 %collective-permute-done.1 = bf16[1,6,3584]{2,1,0:T(8,128)(2,1)S(1)} collective-permute-done((bf16[1,6,3584]{2,1,0:T(8,128)(2,1)S(1)}, bf16[1,6,3584]{2,1,0:T(8,128)(2,1)S(1)}, u32[]{:S(2)}, u32[]{:S(2)}) %collective-permute-start.1) | collective-permute-done | bytes 43040 | tf_op jit(solution)/shard_map/ppermute | solution.py:89
  45.7 4.4 %collective-permute-done.2 = bf16[1,6,3584]{2,1,0:T(8,128)(2,1)S(1)} collective-permute-done((bf16[1,6,3584]{2,1,0:T(8,128)(2,1)S(1)}, bf16[1,6,3584]{2,1,0:T(8,128)(2,1)S(1)}, u32[]{:S(2)}, u32[]{:S(2)}) %collective-permute-start.2) | collective-permute-done | bytes 43040 | tf_op jit(solution)/shard_map/ppermute | solution.py:89
  50.1 6.6 %collective-permute-start.3 = (bf16[1,6,3584]{2,1,0:T(8,128)(2,1)S(1)}, bf16[1,6,3584]{2,1,0:T(8,128)(2,1)S(1)}, u32[]{:S(2)}, u32[]{:S(2)}) collective-permute-start(bf16[1,6,3584]{2,1,0:T(8,128)(2,1)S(1)} %get-tuple-element.15), channel_id=1, source_target_pairs={{0,4},{1,5},{2,6},{3,7},{4,0},{5,1},{6,2},{7,3},{8,12},{9,13},{10,... | collective-permute-start | bytes 129032 | tf_op jit(solution)/shard_map/ppermute | solution.py:89
  56.7 3.3 %collective-permute-done.3 = bf16[1,6,3584]{2,1,0:T(8,128)(2,1)S(1)} collective-permute-done((bf16[1,6,3584]{2,1,0:T(8,128)(2,1)S(1)}, bf16[1,6,3584]{2,1,0:T(8,128)(2,1)S(1)}, u32[]{:S(2)}, u32[]{:S(2)}) %collective-permute-start.3) | collective-permute-done | bytes 43040 | tf_op jit(solution)/shard_map/ppermute | solution.py:89
  60.0 3.9 %collective-permute-done.4 = bf16[1,6,3584]{2,1,0:T(8,128)(2,1)S(1)} collective-permute-done((bf16[1,6,3584]{2,1,0:T(8,128)(2,1)S(1)}, bf16[1,6,3584]{2,1,0:T(8,128)(2,1)S(1)}, u32[]{:S(2)}, u32[]{:S(2)}) %collective-permute-start.4) | collective-permute-done | bytes 43040 | tf_op jit(solution)/shard_map/ppermute | solution.py:89
  64.0 4.9 %collective-permute-start.5 = (bf16[1,6,3584]{2,1,0:T(8,128)(2,1)S(1)}, bf16[1,6,3584]{2,1,0:T(8,128)(2,1)S(1)}, u32[]{:S(2)}, u32[]{:S(2)}) collective-permute-start(bf16[1,6,3584]{2,1,0:T(8,128)(2,1)S(1)} %get-tuple-element.13), channel_id=1, source_target_pairs={{0,6},{1,7},{2,4},{3,5},{4,2},{5,3},{6,0},{7,1},{8,14},{9,15},{10,... | collective-permute-start | bytes 129032 | tf_op jit(solution)/shard_map/ppermute | solution.py:89
  68.8 2.1 %collective-permute-done.5 = bf16[1,6,3584]{2,1,0:T(8,128)(2,1)S(1)} collective-permute-done((bf16[1,6,3584]{2,1,0:T(8,128)(2,1)S(1)}, bf16[1,6,3584]{2,1,0:T(8,128)(2,1)S(1)}, u32[]{:S(2)}, u32[]{:S(2)}) %collective-permute-start.5) | collective-permute-done | bytes 43040 | tf_op jit(solution)/shard_map/ppermute | solution.py:89
  71.0 1.4 collective-permute-start.6
  72.4 3.1 %collective-permute-done.6 = bf16[1,6,3584]{2,1,0:T(8,128)(2,1)S(1)} collective-permute-done((bf16[1,6,3584]{2,1,0:T(8,128)(2,1)S(1)}, bf16[1,6,3584]{2,1,0:T(8,128)(2,1)S(1)}, u32[]{:S(2)}, u32[]{:S(2)}) %collective-permute-start.6) | collective-permute-done | bytes 43040 | tf_op jit(solution)/shard_map/ppermute | solution.py:89
  75.5 1.8 %collective-permute-start.7 = (bf16[1,6,3584]{2,1,0:T(8,128)(2,1)S(1)}, bf16[1,6,3584]{2,1,0:T(8,128)(2,1)S(1)}, u32[]{:S(2)}, u32[]{:S(2)}) collective-permute-start(bf16[1,6,3584]{2,1,0:T(8,128)(2,1)S(1)} %get-tuple-element.11), channel_id=1, source_target_pairs={{0,8},{1,9},{2,10},{3,11},{4,12},{5,13},{6,14},{7,15},{8,0},{9,1},... | collective-permute-start | bytes 129032 | tf_op jit(solution)/shard_map/ppermute | solution.py:89
  77.4 3.3 %collective-permute-done.7 = bf16[1,6,3584]{2,1,0:T(8,128)(2,1)S(1)} collective-permute-done((bf16[1,6,3584]{2,1,0:T(8,128)(2,1)S(1)}, bf16[1,6,3584]{2,1,0:T(8,128)(2,1)S(1)}, u32[]{:S(2)}, u32[]{:S(2)}) %collective-permute-start.7) | collective-permute-done | bytes 43040 | tf_op jit(solution)/shard_map/ppermute | solution.py:89
  80.7 4.8 %collective-permute-done.8 = bf16[1,6,3584]{2,1,0:T(8,128)(2,1)S(1)} collective-permute-done((bf16[1,6,3584]{2,1,0:T(8,128)(2,1)S(1)}, bf16[1,6,3584]{2,1,0:T(8,128)(2,1)S(1)}, u32[]{:S(2)}, u32[]{:S(2)}) %collective-permute-start.8) | collective-permute-done | bytes 43040 | tf_op jit(solution)/shard_map/ppermute | solution.py:89
  85.5 3.5 %collective-permute-start.9 = (bf16[1,6,3584]{2,1,0:T(8,128)(2,1)S(1)}, bf16[1,6,3584]{2,1,0:T(8,128)(2,1)S(1)}, u32[]{:S(2)}, u32[]{:S(2)}) collective-permute-start(bf16[1,6,3584]{2,1,0:T(8,128)(2,1)S(1)} %get-tuple-element.9), channel_id=1, source_target_pairs={{0,10},{1,11},{2,8},{3,9},{4,14},{5,15},{6,12},{7,13},{8,2},{9,3},... | collective-permute-start | bytes 129032 | tf_op jit(solution)/shard_map/ppermute | solution.py:89
  89.0 2.5 %collective-permute-done.9 = bf16[1,6,3584]{2,1,0:T(8,128)(2,1)S(1)} collective-permute-done((bf16[1,6,3584]{2,1,0:T(8,128)(2,1)S(1)}, bf16[1,6,3584]{2,1,0:T(8,128)(2,1)S(1)}, u32[]{:S(2)}, u32[]{:S(2)}) %collective-permute-start.9) | collective-permute-done | bytes 43040 | tf_op jit(solution)/shard_map/ppermute | solution.py:89
  91.5 5.8 %collective-permute-done.10 = bf16[1,6,3584]{2,1,0:T(8,128)(2,1)S(1)} collective-permute-done((bf16[1,6,3584]{2,1,0:T(8,128)(2,1)S(1)}, bf16[1,6,3584]{2,1,0:T(8,128)(2,1)S(1)}, u32[]{:S(2)}, u32[]{:S(2)}) %collective-permute-start.10) | collective-permute-done | bytes 43040 | tf_op jit(solution)/shard_map/ppermute | solution.py:89
  97.4 0.2 reshape.108
  97.6 2.9 %fusion.3 = f32[96,512]{1,0:T(8,128)S(1)} fusion(bf16[96,3584]{1,0:T(8,128)(2,1)S(1)} %reshape.108, bf16[1,3584,512]{2,1,0:T(8,128)(2,1)} %param.11), kind=kOutput, calls=%fused_computation.11 | convolution fusion | flops 352321536 | bytes 4554752 | tf_op jit(solution)/shard_map/dot_general | solution.py:10
  100.8 0.7 fusion.6
  101.8 3.4 %fusion.8 = f32[96,512]{1,0:T(8,128)S(1)} fusion(bf16[96,3584]{1,0:T(8,128)(2,1)S(1)} %reshape.106, bf16[1,512,3584]{2,1,0:T(8,128)(2,1)} %param.13), kind=kOutput, calls=%fused_computation.16 | convolution fusion | flops 352321536 | bytes 4554752 | tf_op jit(solution)/shard_map/dot_general | solution.py:15
  105.2 1.2 fusion.1
  106.4 0.8 copy-done.2
  107.2 1.2 fusion
  108.5 1.2 reshape.109
  109.6 6.4 %all-to-all-start.1 = ((bf16[16,6,3584]{2,1,0:T(8,128)(2,1)}), bf16[16,6,3584]{2,1,0:T(8,128)(2,1)S(1)}, u32[]{:S(2)}, u32[]{:S(2)}) async-start(bf16[16,6,3584]{2,1,0:T(8,128)(2,1)} %reshape.109), calls=%async_computation.1 | async-start | bytes 1835008 | tf_op jit(solution)/shard_map/all_to_all | solution.py:110
  116.1 0.6 dynamic-slice
  117.3 0.8 scatter_custom_fusion
  118.1 4.2 %convolution_bitcast_fusion = f32[1,512,3584]{2,1,0:T(8,128)} fusion(bf16[96,3584]{1,0:T(8,128)(2,1)S(1)} %reshape.106, f32[96,512]{1,0:T(8,128)S(1)} %fusion.6, f32[96,512]{1,0:T(8,128)S(1)} %fusion.3), kind=kOutput, calls=%fused_computation.5 | convolution fusion | flops 352616448 | bytes 8421376 | tf_op jit(solution)/shard_map/dot_general | solution.py:29
  122.3 16.1 %all-to-all-done.1 = bf16[16,6,3584]{2,1,0:T(8,128)(2,1)S(1)} async-done(((bf16[16,6,3584]{2,1,0:T(8,128)(2,1)}), bf16[16,6,3584]{2,1,0:T(8,128)(2,1)S(1)}, u32[]{:S(2)}, u32[]{:S(2)}) %all-to-all-start.1) | async-done | bytes 688160 | tf_op jit(solution)/shard_map/all_to_all | solution.py:110
  138.8 9.0 %all-reduce = bf16[8,3584]{1,0:T(8,128)(2,1)S(1)} all-reduce(bf16[8,3584]{1,0:T(8,128)(2,1)S(1)} %convolution_convert_fusion), channel_id=2, replica_groups=mesh['sp'=2,'ep'=16] {'sp'}, use_global_device_ids=true, to_apply=%region_5.6.clone | all-reduce | flops 28672 | bytes 114688
  147.8 0.6 dynamic-slice_bitcast_fusion
  (53 shorter events, 2.0 us)
Async XLA Ops:
  0.6 20.5 %copy-start.3 = (bf16[1,4,3584]{2,1,0:T(4,128)(2,1)S(1)}, bf16[1,4,3584]{2,1,0:T(4,128)(2,1)}, u32[]{:S(2)}) copy-start(bf16[1,4,3584]{2,1,0:T(4,128)(2,1)} %param.8) | copy-start | bytes 86020
  16.6 24.1 %collective-permute-start = (bf16[1,6,3584]{2,1,0:T(8,128)(2,1)S(1)}, bf16[1,6,3584]{2,1,0:T(8,128)(2,1)S(1)}, u32[]{:S(2)}, u32[]{:S(2)}) collective-permute-start(bf16[1,6,3584]{2,1,0:T(8,128)(2,1)S(1)} %get-tuple-element.18), channel_id=1, source_target_pairs={{0,1},{1,0},{2,3},{3,2},{4,5},{5,4},{6,7},{7,6},{8,9},{9,8},{10,11... | collective-permute-start | bytes 129032 | tf_op jit(solution)/shard_map/ppermute | solution.py:89
  30.1 71.4 %all-to-all-start = ((bf16[16,6,3584]{2,1,0:T(8,128)(2,1)}), bf16[16,6,3584]{2,1,0:T(8,128)(2,1)S(1)}, u32[]{:S(2)}, u32[]{:S(2)}) async-start(bf16[16,6,3584]{2,1,0:T(8,128)(2,1)} %reshape.105), calls=%async_computation | async-start | bytes 1835008 | tf_op jit(solution)/shard_map/all_to_all | solution.py:99
  36.3 61.1 %collective-permute-start.14 = (bf16[1,6,3584]{2,1,0:T(8,128)(2,1)S(1)}, bf16[1,6,3584]{2,1,0:T(8,128)(2,1)S(1)}, u32[]{:S(2)}, u32[]{:S(2)}) collective-permute-start(bf16[1,6,3584]{2,1,0:T(8,128)(2,1)S(1)} %get-tuple-element.4), channel_id=1, source_target_pairs={{0,15},{1,14},{2,13},{3,12},{4,11},{5,10},{6,9},{7,8},{8,7},{9,6},... | collective-permute-start | bytes 129032 | tf_op jit(solution)/shard_map/ppermute | solution.py:89
  37.5 59.9 %collective-permute-start.13 = (bf16[1,6,3584]{2,1,0:T(8,128)(2,1)S(1)}, bf16[1,6,3584]{2,1,0:T(8,128)(2,1)S(1)}, u32[]{:S(2)}, u32[]{:S(2)}) collective-permute-start(bf16[1,6,3584]{2,1,0:T(8,128)(2,1)S(1)} %get-tuple-element.5), channel_id=1, source_target_pairs={{0,14},{1,15},{2,12},{3,13},{4,10},{5,11},{6,8},{7,9},{8,6},{9,7},... | collective-permute-start | bytes 129032 | tf_op jit(solution)/shard_map/ppermute | solution.py:89
  38.9 58.4 %collective-permute-start.12 = (bf16[1,6,3584]{2,1,0:T(8,128)(2,1)S(1)}, bf16[1,6,3584]{2,1,0:T(8,128)(2,1)S(1)}, u32[]{:S(2)}, u32[]{:S(2)}) collective-permute-start(bf16[1,6,3584]{2,1,0:T(8,128)(2,1)S(1)} %get-tuple-element.6), channel_id=1, source_target_pairs={{0,13},{1,12},{2,15},{3,14},{4,9},{5,8},{6,11},{7,10},{8,5},{9,4},... | collective-permute-start | bytes 129032 | tf_op jit(solution)/shard_map/ppermute | solution.py:89
  39.2 58.1 %collective-permute-start.11 = (bf16[1,6,3584]{2,1,0:T(8,128)(2,1)S(1)}, bf16[1,6,3584]{2,1,0:T(8,128)(2,1)S(1)}, u32[]{:S(2)}, u32[]{:S(2)}) collective-permute-start(bf16[1,6,3584]{2,1,0:T(8,128)(2,1)S(1)} %get-tuple-element.7), channel_id=1, source_target_pairs={{0,12},{1,13},{2,14},{3,15},{4,8},{5,9},{6,10},{7,11},{8,4},{9,5},... | collective-permute-start | bytes 129032 | tf_op jit(solution)/shard_map/ppermute | solution.py:89
  40.7 5.0 %collective-permute-start.1 = (bf16[1,6,3584]{2,1,0:T(8,128)(2,1)S(1)}, bf16[1,6,3584]{2,1,0:T(8,128)(2,1)S(1)}, u32[]{:S(2)}, u32[]{:S(2)}) collective-permute-start(bf16[1,6,3584]{2,1,0:T(8,128)(2,1)S(1)} %get-tuple-element.17), channel_id=1, source_target_pairs={{0,2},{1,3},{2,0},{3,1},{4,6},{5,7},{6,4},{7,5},{8,10},{9,11},{10,... | collective-permute-start | bytes 129032 | tf_op jit(solution)/shard_map/ppermute | solution.py:89
  45.7 4.4 %collective-permute-start.2 = (bf16[1,6,3584]{2,1,0:T(8,128)(2,1)S(1)}, bf16[1,6,3584]{2,1,0:T(8,128)(2,1)S(1)}, u32[]{:S(2)}, u32[]{:S(2)}) collective-permute-start(bf16[1,6,3584]{2,1,0:T(8,128)(2,1)S(1)} %get-tuple-element.16), channel_id=1, source_target_pairs={{0,3},{1,2},{2,1},{3,0},{4,7},{5,6},{6,5},{7,4},{8,11},{9,10},{10,... | collective-permute-start | bytes 129032 | tf_op jit(solution)/shard_map/ppermute | solution.py:89
  50.1 9.9 %collective-permute-start.3 = (bf16[1,6,3584]{2,1,0:T(8,128)(2,1)S(1)}, bf16[1,6,3584]{2,1,0:T(8,128)(2,1)S(1)}, u32[]{:S(2)}, u32[]{:S(2)}) collective-permute-start(bf16[1,6,3584]{2,1,0:T(8,128)(2,1)S(1)} %get-tuple-element.15), channel_id=1, source_target_pairs={{0,4},{1,5},{2,6},{3,7},{4,0},{5,1},{6,2},{7,3},{8,12},{9,13},{10,... | collective-permute-start | bytes 129032 | tf_op jit(solution)/shard_map/ppermute | solution.py:89
  60.0 3.9 %collective-permute-start.4 = (bf16[1,6,3584]{2,1,0:T(8,128)(2,1)S(1)}, bf16[1,6,3584]{2,1,0:T(8,128)(2,1)S(1)}, u32[]{:S(2)}, u32[]{:S(2)}) collective-permute-start(bf16[1,6,3584]{2,1,0:T(8,128)(2,1)S(1)} %get-tuple-element.14), channel_id=1, source_target_pairs={{0,5},{1,4},{2,7},{3,6},{4,1},{5,0},{6,3},{7,2},{8,13},{9,12},{10,... | collective-permute-start | bytes 129032 | tf_op jit(solution)/shard_map/ppermute | solution.py:89
  64.0 7.0 %collective-permute-start.5 = (bf16[1,6,3584]{2,1,0:T(8,128)(2,1)S(1)}, bf16[1,6,3584]{2,1,0:T(8,128)(2,1)S(1)}, u32[]{:S(2)}, u32[]{:S(2)}) collective-permute-start(bf16[1,6,3584]{2,1,0:T(8,128)(2,1)S(1)} %get-tuple-element.13), channel_id=1, source_target_pairs={{0,6},{1,7},{2,4},{3,5},{4,2},{5,3},{6,0},{7,1},{8,14},{9,15},{10,... | collective-permute-start | bytes 129032 | tf_op jit(solution)/shard_map/ppermute | solution.py:89
  71.0 4.5 %collective-permute-start.6 = (bf16[1,6,3584]{2,1,0:T(8,128)(2,1)S(1)}, bf16[1,6,3584]{2,1,0:T(8,128)(2,1)S(1)}, u32[]{:S(2)}, u32[]{:S(2)}) collective-permute-start(bf16[1,6,3584]{2,1,0:T(8,128)(2,1)S(1)} %get-tuple-element.12), channel_id=1, source_target_pairs={{0,7},{1,6},{2,5},{3,4},{4,3},{5,2},{6,1},{7,0},{8,15},{9,14},{10,... | collective-permute-start | bytes 129032 | tf_op jit(solution)/shard_map/ppermute | solution.py:89
  75.5 5.1 %collective-permute-start.7 = (bf16[1,6,3584]{2,1,0:T(8,128)(2,1)S(1)}, bf16[1,6,3584]{2,1,0:T(8,128)(2,1)S(1)}, u32[]{:S(2)}, u32[]{:S(2)}) collective-permute-start(bf16[1,6,3584]{2,1,0:T(8,128)(2,1)S(1)} %get-tuple-element.11), channel_id=1, source_target_pairs={{0,8},{1,9},{2,10},{3,11},{4,12},{5,13},{6,14},{7,15},{8,0},{9,1},... | collective-permute-start | bytes 129032 | tf_op jit(solution)/shard_map/ppermute | solution.py:89
  80.7 4.8 %collective-permute-start.8 = (bf16[1,6,3584]{2,1,0:T(8,128)(2,1)S(1)}, bf16[1,6,3584]{2,1,0:T(8,128)(2,1)S(1)}, u32[]{:S(2)}, u32[]{:S(2)}) collective-permute-start(bf16[1,6,3584]{2,1,0:T(8,128)(2,1)S(1)} %get-tuple-element.10), channel_id=1, source_target_pairs={{0,9},{1,8},{2,11},{3,10},{4,13},{5,12},{6,15},{7,14},{8,1},{9,0},... | collective-permute-start | bytes 129032 | tf_op jit(solution)/shard_map/ppermute | solution.py:89
  85.5 6.0 %collective-permute-start.9 = (bf16[1,6,3584]{2,1,0:T(8,128)(2,1)S(1)}, bf16[1,6,3584]{2,1,0:T(8,128)(2,1)S(1)}, u32[]{:S(2)}, u32[]{:S(2)}) collective-permute-start(bf16[1,6,3584]{2,1,0:T(8,128)(2,1)S(1)} %get-tuple-element.9), channel_id=1, source_target_pairs={{0,10},{1,11},{2,8},{3,9},{4,14},{5,15},{6,12},{7,13},{8,2},{9,3},... | collective-permute-start | bytes 129032 | tf_op jit(solution)/shard_map/ppermute | solution.py:89
  91.5 5.8 %collective-permute-start.10 = (bf16[1,6,3584]{2,1,0:T(8,128)(2,1)S(1)}, bf16[1,6,3584]{2,1,0:T(8,128)(2,1)S(1)}, u32[]{:S(2)}, u32[]{:S(2)}) collective-permute-start(bf16[1,6,3584]{2,1,0:T(8,128)(2,1)S(1)} %get-tuple-element.8), channel_id=1, source_target_pairs={{0,11},{1,10},{2,9},{3,8},{4,15},{5,14},{6,13},{7,12},{8,3},{9,2},... | collective-permute-start | bytes 129032 | tf_op jit(solution)/shard_map/ppermute | solution.py:89
  97.6 3.1 %copy-start.1 = (bf16[1,3584,512]{2,1,0:T(8,128)(2,1)S(1)}, bf16[1,3584,512]{2,1,0:T(8,128)(2,1)}, u32[]{:S(2)}) copy-start(bf16[1,3584,512]{2,1,0:T(8,128)(2,1)} %param.12) | copy-start | bytes 11010052
  101.7 3.4 %copy-start = (bf16[1,3584,512]{2,1,0:T(8,128)(2,1)S(1)}, bf16[1,3584,512]{2,1,0:T(8,128)(2,1)}, u32[]{:S(2)}) copy-start(bf16[1,3584,512]{2,1,0:T(8,128)(2,1)} %param.11) | copy-start | bytes 11010052
  105.2 2.0 %copy-start.2 = (bf16[1,3584,512]{2,1,0:T(8,128)(2,1)S(1)}, bf16[1,3584,512]{2,1,0:T(8,128)(2,1)}, u32[]{:S(2)}) copy-start(bf16[1,3584,512]{2,1,0:T(8,128)(2,1)} %param.12) | copy-start | bytes 11010052
  107.2 8.9 %copy-start.4 = (u32[32]{0:T(128)S(1)}, u32[32]{0:T(128)}, u32[]{:S(2)}) copy-start(u32[32]{0:T(128)} %constant.77) | copy-start | bytes 388
  109.6 28.8 %all-to-all-start.1 = ((bf16[16,6,3584]{2,1,0:T(8,128)(2,1)}), bf16[16,6,3584]{2,1,0:T(8,128)(2,1)S(1)}, u32[]{:S(2)}, u32[]{:S(2)}) async-start(bf16[16,6,3584]{2,1,0:T(8,128)(2,1)} %reshape.109), calls=%async_computation.1 | async-start | bytes 1835008 | tf_op jit(solution)/shard_map/all_to_all | solution.py:110
